TPU v7x, 512 devices: a whole 4x4x16 slice. The times are simulated.
512 devices in a mesh: prow: 16 (over y, x), pcol: 32 (over z, core).
Axes of the slice: x: 4, y: 4, z: 16, core: 2. Of those that a mesh axis runs over, the one named last changes fastest.
Arguments:
- factor_tiles: bfloat16 [16, 1024, 1, 16, 1024], P(None, 'pcol', None, 'prow'), may hold values from -0.03125 to 0.03125
- inverse_blocks: bfloat16 [1, 16, 1024, 1024], P(None, 'prow'), may hold values from -1 to 3, as said below
- demand: bfloat16 [16, 1024, 256], P(None, 'pcol'), may hold values from -6 to 6
Outputs:
- solved: bfloat16 [1, 16, 1024, 256], P(None, 'prow')
Inputs may be any that keep to these rules, and one draw needn't show every extreme that they name: `inverse_blocks`: each [1024, 1024] block is lower triangular with a positive diagonal.
All inputs are finite; a program needn't handle non-finite values.
Results may differ from a plain program's by a relative error of at most 0.0075.
Values may be sent and summed in bfloat16 or wider, within the bound.
A program may use at most 64 MiB of HBM per device.

v0:
```python
import jax
import jax.numpy as jnp
from jax import lax
from jax.sharding import PartitionSpec as P


def on_device(factor_tiles, inverse_blocks, demand):
    block_count, slice_rows, col_slots, single, block_width = factor_tiles.shape
    columns = demand.shape[2]
    prow_size = lax.axis_size("prow")
    my_row = lax.axis_index("prow")
    row_tiles = factor_tiles.reshape(block_count, slice_rows, col_slots * block_width)
    inverse = inverse_blocks.reshape(col_slots, block_width, block_width)
    owned_blocks = jnp.zeros((col_slots, block_width, columns), jnp.bfloat16)
    pending = jnp.zeros((block_count, slice_rows, columns), jnp.float32)

    def advance(step_index, carried):
        owned_blocks, pending = carried
        owner_row = step_index % prow_size
        slot_index = step_index // prow_size
        is_owner = my_row == owner_row
        partial_sum = lax.dynamic_index_in_dim(pending, step_index, 0, keepdims=False)
        summed = lax.psum(partial_sum, "prow")
        target = lax.dynamic_index_in_dim(demand, step_index, 0, keepdims=False)
        residual = (target.astype(jnp.float32) - summed).astype(jnp.bfloat16)
        block_inv = lax.dynamic_index_in_dim(inverse, slot_index, 0, keepdims=False)
        apply_running = jnp.zeros((block_width, columns), jnp.float32)
        segment = lax.all_gather(residual, "pcol", axis=0, tiled=True)
        solved = lax.cond(
            is_owner,
            lambda: jnp.dot(block_inv, segment, preferred_element_type=jnp.float32),
            lambda: apply_running,
        ).astype(jnp.bfloat16)
        owned_blocks = jnp.where(
            is_owner,
            lax.dynamic_update_index_in_dim(owned_blocks, solved, slot_index, 0),
            owned_blocks,
        )
        pending = lax.cond(
            is_owner,
            lambda running: running
            + jnp.einsum("krw,wn->krn", row_tiles, solved, preferred_element_type=jnp.float32),
            lambda running: running,
            pending,
        )
        return (owned_blocks, pending)

    owned_blocks, pending = lax.fori_loop(0, block_count, advance, (owned_blocks, pending))
    return owned_blocks.reshape(col_slots, 1, block_width, columns)


def solution(mesh):
    placed = (
        P(None, "pcol", None, "prow", None),
        P(None, "prow", None, None),
        P(None, "pcol", None),
    )
    return jax.shard_map(
        on_device,
        mesh=mesh,
        in_specs=placed,
        out_specs=P(None, "prow", None, None),
        check_vma=False,
    )
```

profile of v0, /device:TPU:1, one launch (start us, length us, event | category | flops | bytes accessed | tf_op | source)
XLA Modules:
  0.0 1639.2 jit_solution(5200162110590774931)
XLA Ops:
  0.1 1638.4 %while.21 = (s32[]{:T(128)}, bf16[1,1024,256]{2,1,0:T(8,128)(2,1)S(1)}, f32[16,32,256]{2,1,0:T(8,128)S(1)}, s32[]{:T(128)}, bf16[16,32,256]{2,1,0:T(8,128)(2,1)}...) while((s32[]{:T(128)}, ...), condition=%wide.region_6.7_spmd.clone, body=%wide.region_0.6_spmd.clone.sunk | while | flops 806256640 | bytes 13320484 | solution.py:48
  0.1 61.6 %psum.16 = f32[32,256]{1,0:T(8,128)S(1)} all-reduce(f32[32,256]{1,0:T(8,128)S(1)} %dynamic-slice_bitcast_fusion.2), channel_id=1, replica_groups=mesh['prow'=16,'pcol'=32] {'prow'}, use_global_device_ids=true, to_apply=%region_1.1 | all-reduce | flops 8192 | bytes 65536 | tf_op jit(solution)/shard_map/while/body/eval_jaxpr/psum | solution.py:23
  62.4 52.0 %all_gather.12 = bf16[1024,256]{1,0:T(8,128)(2,1)S(1)} all-gather(bf16[32,256]{1,0:T(8,128)(2,1)S(1)} %fusion.10), channel_id=1, replica_groups=mesh['prow'=16,'pcol'=32] {'pcol'}, dimensions={0}, use_global_device_ids=true | all-gather | bytes 540672 | tf_op jit(solution)/shard_map/while/body/eval_jaxpr/all_gather | solution.py:28
  114.4 4.2 conditional.6
  114.4 3.2 fusion.2
  117.6 1.0 copy.7
  118.6 1.5 conditional.7
  118.6 1.5 convolution_add_fusion
  120.4 55.8 %psum.16 = f32[32,256]{1,0:T(8,128)S(1)} all-reduce(f32[32,256]{1,0:T(8,128)S(1)} %dynamic-slice_bitcast_fusion.2), channel_id=1, replica_groups=mesh['prow'=16,'pcol'=32] {'prow'}, use_global_device_ids=true, to_apply=%region_1.1 | all-reduce | flops 8192 | bytes 65536 | tf_op jit(solution)/shard_map/while/body/eval_jaxpr/psum | solution.py:23
  176.9 42.0 %all_gather.12 = bf16[1024,256]{1,0:T(8,128)(2,1)S(1)} all-gather(bf16[32,256]{1,0:T(8,128)(2,1)S(1)} %fusion.10), channel_id=1, replica_groups=mesh['prow'=16,'pcol'=32] {'pcol'}, dimensions={0}, use_global_device_ids=true | all-gather | bytes 540672 | tf_op jit(solution)/shard_map/while/body/eval_jaxpr/all_gather | solution.py:28
  218.8 0.9 conditional.6
  218.8 0.8 broadcast.8
  220.5 58.3 %psum.16 = f32[32,256]{1,0:T(8,128)S(1)} all-reduce(f32[32,256]{1,0:T(8,128)S(1)} %dynamic-slice_bitcast_fusion.2), channel_id=1, replica_groups=mesh['prow'=16,'pcol'=32] {'prow'}, use_global_device_ids=true, to_apply=%region_1.1 | all-reduce | flops 8192 | bytes 65536 | tf_op jit(solution)/shard_map/while/body/eval_jaxpr/psum | solution.py:23
  279.5 44.1 %all_gather.12 = bf16[1024,256]{1,0:T(8,128)(2,1)S(1)} all-gather(bf16[32,256]{1,0:T(8,128)(2,1)S(1)} %fusion.10), channel_id=1, replica_groups=mesh['prow'=16,'pcol'=32] {'pcol'}, dimensions={0}, use_global_device_ids=true | all-gather | bytes 540672 | tf_op jit(solution)/shard_map/while/body/eval_jaxpr/all_gather | solution.py:28
  323.6 0.9 conditional.6
  323.6 0.8 broadcast.8
  325.3 55.8 %psum.16 = f32[32,256]{1,0:T(8,128)S(1)} all-reduce(f32[32,256]{1,0:T(8,128)S(1)} %dynamic-slice_bitcast_fusion.2), channel_id=1, replica_groups=mesh['prow'=16,'pcol'=32] {'prow'}, use_global_device_ids=true, to_apply=%region_1.1 | all-reduce | flops 8192 | bytes 65536 | tf_op jit(solution)/shard_map/while/body/eval_jaxpr/psum | solution.py:23
  381.8 42.0 %all_gather.12 = bf16[1024,256]{1,0:T(8,128)(2,1)S(1)} all-gather(bf16[32,256]{1,0:T(8,128)(2,1)S(1)} %fusion.10), channel_id=1, replica_groups=mesh['prow'=16,'pcol'=32] {'pcol'}, dimensions={0}, use_global_device_ids=true | all-gather | bytes 540672 | tf_op jit(solution)/shard_map/while/body/eval_jaxpr/all_gather | solution.py:28
  423.8 0.9 conditional.6
  423.8 0.8 broadcast.8
  425.4 55.8 %psum.16 = f32[32,256]{1,0:T(8,128)S(1)} all-reduce(f32[32,256]{1,0:T(8,128)S(1)} %dynamic-slice_bitcast_fusion.2), channel_id=1, replica_groups=mesh['prow'=16,'pcol'=32] {'prow'}, use_global_device_ids=true, to_apply=%region_1.1 | all-reduce | flops 8192 | bytes 65536 | tf_op jit(solution)/shard_map/while/body/eval_jaxpr/psum | solution.py:23
  481.9 43.9 %all_gather.12 = bf16[1024,256]{1,0:T(8,128)(2,1)S(1)} all-gather(bf16[32,256]{1,0:T(8,128)(2,1)S(1)} %fusion.10), channel_id=1, replica_groups=mesh['prow'=16,'pcol'=32] {'pcol'}, dimensions={0}, use_global_device_ids=true | all-gather | bytes 540672 | tf_op jit(solution)/shard_map/while/body/eval_jaxpr/all_gather | solution.py:28
  525.8 0.9 conditional.6
  525.8 0.8 broadcast.8
  527.5 55.8 %psum.16 = f32[32,256]{1,0:T(8,128)S(1)} all-reduce(f32[32,256]{1,0:T(8,128)S(1)} %dynamic-slice_bitcast_fusion.2), channel_id=1, replica_groups=mesh['prow'=16,'pcol'=32] {'prow'}, use_global_device_ids=true, to_apply=%region_1.1 | all-reduce | flops 8192 | bytes 65536 | tf_op jit(solution)/shard_map/while/body/eval_jaxpr/psum | solution.py:23
  584.0 42.0 %all_gather.12 = bf16[1024,256]{1,0:T(8,128)(2,1)S(1)} all-gather(bf16[32,256]{1,0:T(8,128)(2,1)S(1)} %fusion.10), channel_id=1, replica_groups=mesh['prow'=16,'pcol'=32] {'pcol'}, dimensions={0}, use_global_device_ids=true | all-gather | bytes 540672 | tf_op jit(solution)/shard_map/while/body/eval_jaxpr/all_gather | solution.py:28
  625.9 0.9 conditional.6
  625.9 0.8 broadcast.8
  627.6 55.8 %psum.16 = f32[32,256]{1,0:T(8,128)S(1)} all-reduce(f32[32,256]{1,0:T(8,128)S(1)} %dynamic-slice_bitcast_fusion.2), channel_id=1, replica_groups=mesh['prow'=16,'pcol'=32] {'prow'}, use_global_device_ids=true, to_apply=%region_1.1 | all-reduce | flops 8192 | bytes 65536 | tf_op jit(solution)/shard_map/while/body/eval_jaxpr/psum | solution.py:23
  684.1 43.9 %all_gather.12 = bf16[1024,256]{1,0:T(8,128)(2,1)S(1)} all-gather(bf16[32,256]{1,0:T(8,128)(2,1)S(1)} %fusion.10), channel_id=1, replica_groups=mesh['prow'=16,'pcol'=32] {'pcol'}, dimensions={0}, use_global_device_ids=true | all-gather | bytes 540672 | tf_op jit(solution)/shard_map/while/body/eval_jaxpr/all_gather | solution.py:28
  728.0 0.9 conditional.6
  728.0 0.8 broadcast.8
  729.7 55.8 %psum.16 = f32[32,256]{1,0:T(8,128)S(1)} all-reduce(f32[32,256]{1,0:T(8,128)S(1)} %dynamic-slice_bitcast_fusion.2), channel_id=1, replica_groups=mesh['prow'=16,'pcol'=32] {'prow'}, use_global_device_ids=true, to_apply=%region_1.1 | all-reduce | flops 8192 | bytes 65536 | tf_op jit(solution)/shard_map/while/body/eval_jaxpr/psum | solution.py:23
  786.1 42.0 %all_gather.12 = bf16[1024,256]{1,0:T(8,128)(2,1)S(1)} all-gather(bf16[32,256]{1,0:T(8,128)(2,1)S(1)} %fusion.10), channel_id=1, replica_groups=mesh['prow'=16,'pcol'=32] {'pcol'}, dimensions={0}, use_global_device_ids=true | all-gather | bytes 540672 | tf_op jit(solution)/shard_map/while/body/eval_jaxpr/all_gather | solution.py:28
  828.1 0.9 conditional.6
  828.1 0.8 broadcast.8
  829.8 55.8 %psum.16 = f32[32,256]{1,0:T(8,128)S(1)} all-reduce(f32[32,256]{1,0:T(8,128)S(1)} %dynamic-slice_bitcast_fusion.2), channel_id=1, replica_groups=mesh['prow'=16,'pcol'=32] {'prow'}, use_global_device_ids=true, to_apply=%region_1.1 | all-reduce | flops 8192 | bytes 65536 | tf_op jit(solution)/shard_map/while/body/eval_jaxpr/psum | solution.py:23
  886.3 43.9 %all_gather.12 = bf16[1024,256]{1,0:T(8,128)(2,1)S(1)} all-gather(bf16[32,256]{1,0:T(8,128)(2,1)S(1)} %fusion.10), channel_id=1, replica_groups=mesh['prow'=16,'pcol'=32] {'pcol'}, dimensions={0}, use_global_device_ids=true | all-gather | bytes 540672 | tf_op jit(solution)/shard_map/while/body/eval_jaxpr/all_gather | solution.py:28
  930.2 0.9 conditional.6
  930.2 0.8 broadcast.8
  931.8 55.8 %psum.16 = f32[32,256]{1,0:T(8,128)S(1)} all-reduce(f32[32,256]{1,0:T(8,128)S(1)} %dynamic-slice_bitcast_fusion.2), channel_id=1, replica_groups=mesh['prow'=16,'pcol'=32] {'prow'}, use_global_device_ids=true, to_apply=%region_1.1 | all-reduce | flops 8192 | bytes 65536 | tf_op jit(solution)/shard_map/while/body/eval_jaxpr/psum | solution.py:23
  988.3 42.0 %all_gather.12 = bf16[1024,256]{1,0:T(8,128)(2,1)S(1)} all-gather(bf16[32,256]{1,0:T(8,128)(2,1)S(1)} %fusion.10), channel_id=1, replica_groups=mesh['prow'=16,'pcol'=32] {'pcol'}, dimensions={0}, use_global_device_ids=true | all-gather | bytes 540672 | tf_op jit(solution)/shard_map/while/body/eval_jaxpr/all_gather | solution.py:28
  1030.3 0.9 conditional.6
  1030.3 0.8 broadcast.8
  1031.9 55.8 %psum.16 = f32[32,256]{1,0:T(8,128)S(1)} all-reduce(f32[32,256]{1,0:T(8,128)S(1)} %dynamic-slice_bitcast_fusion.2), channel_id=1, replica_groups=mesh['prow'=16,'pcol'=32] {'prow'}, use_global_device_ids=true, to_apply=%region_1.1 | all-reduce | flops 8192 | bytes 65536 | tf_op jit(solution)/shard_map/while/body/eval_jaxpr/psum | solution.py:23
  1088.4 43.9 %all_gather.12 = bf16[1024,256]{1,0:T(8,128)(2,1)S(1)} all-gather(bf16[32,256]{1,0:T(8,128)(2,1)S(1)} %fusion.10), channel_id=1, replica_groups=mesh['prow'=16,'pcol'=32] {'pcol'}, dimensions={0}, use_global_device_ids=true | all-gather | bytes 540672 | tf_op jit(solution)/shard_map/while/body/eval_jaxpr/all_gather | solution.py:28
  1132.3 0.9 conditional.6
  1132.3 0.8 broadcast.8
  1134.0 55.8 %psum.16 = f32[32,256]{1,0:T(8,128)S(1)} all-reduce(f32[32,256]{1,0:T(8,128)S(1)} %dynamic-slice_bitcast_fusion.2), channel_id=1, replica_groups=mesh['prow'=16,'pcol'=32] {'prow'}, use_global_device_ids=true, to_apply=%region_1.1 | all-reduce | flops 8192 | bytes 65536 | tf_op jit(solution)/shard_map/while/body/eval_jaxpr/psum | solution.py:23
  1190.5 42.0 %all_gather.12 = bf16[1024,256]{1,0:T(8,128)(2,1)S(1)} all-gather(bf16[32,256]{1,0:T(8,128)(2,1)S(1)} %fusion.10), channel_id=1, replica_groups=mesh['prow'=16,'pcol'=32] {'pcol'}, dimensions={0}, use_global_device_ids=true | all-gather | bytes 540672 | tf_op jit(solution)/shard_map/while/body/eval_jaxpr/all_gather | solution.py:28
  1232.5 0.9 conditional.6
  1234.1 55.8 %psum.16 = f32[32,256]{1,0:T(8,128)S(1)} all-reduce(f32[32,256]{1,0:T(8,128)S(1)} %dynamic-slice_bitcast_fusion.2), channel_id=1, replica_groups=mesh['prow'=16,'pcol'=32] {'prow'}, use_global_device_ids=true, to_apply=%region_1.1 | all-reduce | flops 8192 | bytes 65536 | tf_op jit(solution)/shard_map/while/body/eval_jaxpr/psum | solution.py:23
  1290.6 43.9 %all_gather.12 = bf16[1024,256]{1,0:T(8,128)(2,1)S(1)} all-gather(bf16[32,256]{1,0:T(8,128)(2,1)S(1)} %fusion.10), channel_id=1, replica_groups=mesh['prow'=16,'pcol'=32] {'pcol'}, dimensions={0}, use_global_device_ids=true | all-gather | bytes 540672 | tf_op jit(solution)/shard_map/while/body/eval_jaxpr/all_gather | solution.py:28
  1334.5 0.9 conditional.6
  1336.2 55.8 %psum.16 = f32[32,256]{1,0:T(8,128)S(1)} all-reduce(f32[32,256]{1,0:T(8,128)S(1)} %dynamic-slice_bitcast_fusion.2), channel_id=1, replica_groups=mesh['prow'=16,'pcol'=32] {'prow'}, use_global_device_ids=true, to_apply=%region_1.1 | all-reduce | flops 8192 | bytes 65536 | tf_op jit(solution)/shard_map/while/body/eval_jaxpr/psum | solution.py:23
  1392.7 42.0 %all_gather.12 = bf16[1024,256]{1,0:T(8,128)(2,1)S(1)} all-gather(bf16[32,256]{1,0:T(8,128)(2,1)S(1)} %fusion.10), channel_id=1, replica_groups=mesh['prow'=16,'pcol'=32] {'pcol'}, dimensions={0}, use_global_device_ids=true | all-gather | bytes 540672 | tf_op jit(solution)/shard_map/while/body/eval_jaxpr/all_gather | solution.py:28
  1434.6 0.9 conditional.6
  1436.3 55.8 %psum.16 = f32[32,256]{1,0:T(8,128)S(1)} all-reduce(f32[32,256]{1,0:T(8,128)S(1)} %dynamic-slice_bitcast_fusion.2), channel_id=1, replica_groups=mesh['prow'=16,'pcol'=32] {'prow'}, use_global_device_ids=true, to_apply=%region_1.1 | all-reduce | flops 8192 | bytes 65536 | tf_op jit(solution)/shard_map/while/body/eval_jaxpr/psum | solution.py:23
  1492.8 43.9 %all_gather.12 = bf16[1024,256]{1,0:T(8,128)(2,1)S(1)} all-gather(bf16[32,256]{1,0:T(8,128)(2,1)S(1)} %fusion.10), channel_id=1, replica_groups=mesh['prow'=16,'pcol'=32] {'pcol'}, dimensions={0}, use_global_device_ids=true | all-gather | bytes 540672 | tf_op jit(solution)/shard_map/while/body/eval_jaxpr/all_gather | solution.py:28
  1536.7 0.9 conditional.6
  1538.4 55.8 %psum.16 = f32[32,256]{1,0:T(8,128)S(1)} all-reduce(f32[32,256]{1,0:T(8,128)S(1)} %dynamic-slice_bitcast_fusion.2), channel_id=1, replica_groups=mesh['prow'=16,'pcol'=32] {'prow'}, use_global_device_ids=true, to_apply=%region_1.1 | all-reduce | flops 8192 | bytes 65536 | tf_op jit(solution)/shard_map/while/body/eval_jaxpr/psum | solution.py:23
  1594.8 42.0 %all_gather.12 = bf16[1024,256]{1,0:T(8,128)(2,1)S(1)} all-gather(bf16[32,256]{1,0:T(8,128)(2,1)S(1)} %fusion.10), channel_id=1, replica_groups=mesh['prow'=16,'pcol'=32] {'pcol'}, dimensions={0}, use_global_device_ids=true | all-gather | bytes 540672 | tf_op jit(solution)/shard_map/while/body/eval_jaxpr/all_gather | solution.py:28
  1636.8 0.9 conditional.6
  1636.8 0.8 broadcast.8
  (118 shorter events, 27.7 us)
Async XLA Ops:
  114.4 4.2 copy-start
  218.8 1.4 copy-start
  323.6 1.4 copy-start
  423.8 1.4 copy-start
  525.8 1.4 copy-start
  625.9 1.4 copy-start
  728.0 1.4 copy-start
  828.1 1.4 copy-start
  930.2 1.4 copy-start
  1030.3 1.4 copy-start
  1132.3 1.4 copy-start
  1232.5 1.4 copy-start
  1334.5 1.4 copy-start
  1434.6 1.4 copy-start
  1536.7 1.4 copy-start
  1636.8 1.4 copy-start
  1638.4 0.8 copy-start.1
where the time goes:
time: 1640 us
  blocking collectives  1600 us (98%)
  local copies, waits for them, and re-layouts  23 us (1%)
    psum x16, blocking collectives, advance(): summed = lax.psum(partial_sum, 'prow')  901 us
    all_gather x16, blocking collectives, advance(): segment = lax.all_gather(residual, 'pcol', axis=0, tiled=True)  695 us

commit v1 on v0

v1 whole, which is shorter than its diff:
```python
import functools

import jax
import jax.numpy as jnp
from jax import lax
from jax.experimental import pallas as pl
from jax.experimental.pallas import tpu as pltpu
from jax.sharding import PartitionSpec as P

MESH = pl.DeviceIdType.MESH
NT = (((1,), (1,)), ((), ()))


def dot_nt(lhs, rhs):
    return lax.dot_general(lhs, rhs, NT, preferred_element_type=jnp.float32)


def kernel(
    n, nz, cols, rows,
    tiles, inverse, demand, out,
    gathered, diag, diag_split, asked, base, partial, sol, sol_split, sol_far, contrib, result,
    own_sem, own_send, right_send, right_recv, left_send, left_recv,
    ask_own, ask_rsend, ask_rrecv, ask_lsend, ask_lrecv,
    diag_sem, base_send, base_recv, part_send, part_recv,
    far_send, far_recv, out_send, out_recv, swap_send, swap_recv,
):
    n2, hops = n // 2, nz // 2
    w = lax.axis_index("prow")
    q = lax.axis_index("pcol")
    z, c = q // 2, q % 2
    other = q + 1 - 2 * c
    right = lax.rem(z + 1, nz) * 2 + c
    left = lax.rem(z + nz - 1, nz) * 2 + c
    low = w < n2
    j = jnp.where(low, w, n - 1 - w)
    far = n - 1 - w
    count = jnp.where(low, n2, n2 - 1)
    shared = jnp.where(low, n2 - j, n2 - 1 - j)
    first = jnp.where(low, j + 1, j + 2)
    half = gathered.shape[1] * rows

    def remote(src, dst, send, recv, device):
        return pltpu.make_async_remote_copy(
            src_ref=src, dst_ref=dst, send_sem=send, recv_sem=recv,
            device_id=device, device_id_type=MESH,
        )

    def row_of(k):
        return jnp.where(k < shared, first + 2 * k, jnp.where(low, n2, n2 + 1) + k)

    def is_moved(k):
        return jnp.logical_and(jnp.logical_not(low), k < shared)

    def local_tile(k):
        return pltpu.make_async_copy(tiles.at[row_of(k)], gathered.at[k, z], own_sem.at[k])

    def moved_tile(k, row):
        return remote(tiles.at[row], gathered.at[k, z], own_send.at[k], own_sem.at[k], (far, q))

    def ring_right(k, h):
        o = lax.rem(z - h + nz, nz)
        return remote(gathered.at[k, o], gathered.at[k, o], right_send.at[k, h], right_recv.at[k, h], (w, right))

    def ring_left(k, h):
        o = lax.rem(z + h, nz)
        return remote(gathered.at[k, o], gathered.at[k, o], left_send.at[k, h], left_recv.at[k, h], (w, left))

    def ring_right_in(k, h):
        o = lax.rem(z - h - 1 + nz, nz)
        return remote(gathered.at[k, o], gathered.at[k, o], right_send.at[k, h], right_recv.at[k, h], (w, right))

    def ring_left_in(k, h):
        o = lax.rem(z + h + 1, nz)
        return remote(gathered.at[k, o], gathered.at[k, o], left_send.at[k, h], left_recv.at[k, h], (w, left))

    def ask_right(h):
        o = lax.rem(z - h + nz, nz)
        return remote(asked.at[o], asked.at[o], ask_rsend.at[h], ask_rrecv.at[h], (w, right))

    def ask_left(h):
        o = lax.rem(z + h, nz)
        return remote(asked.at[o], asked.at[o], ask_lsend.at[h], ask_lrecv.at[h], (w, left))

    def ask_right_in(h):
        o = lax.rem(z - h - 1 + nz, nz)
        return remote(asked.at[o], asked.at[o], ask_rsend.at[h], ask_rrecv.at[h], (w, right))

    def ask_left_in(h):
        o = lax.rem(z + h + 1, nz)
        return remote(asked.at[o], asked.at[o], ask_lsend.at[h], ask_lrecv.at[h], (w, left))

    base_copy = remote(base.at[c], base.at[c], base_send, base_recv, (w, other))
    base_in = remote(base.at[1 - c], base.at[1 - c], base_send, base_recv, (w, other))
    far_copy = remote(sol, sol_far, far_send, far_recv, (far, q))
    diag_copy = pltpu.make_async_copy(inverse, diag, diag_sem)
    ask_copy = pltpu.make_async_copy(demand.at[w], asked.at[z], ask_own)

    def part_copy(k, i, col, core):
        return remote(contrib.at[k], partial.at[col, c], part_send.at[k, core], part_recv.at[col, c], (i, 2 * z + core))

    def part_in(col, core):
        return remote(contrib.at[0], partial.at[col, core], part_send.at[0, 0], part_recv.at[col, core], (w, other))

    ask_copy.start()
    for k in range(n2):
        @pl.when(jnp.logical_and(k < count, jnp.logical_not(is_moved(k))))
        def _():
            local_tile(k).start()
    diag_copy.start()

    barrier = pltpu.get_barrier_semaphore()
    me = 2 * w + c

    def greet_plane(d, carry):
        t = lax.rem(me + d, 2 * n)
        pl.semaphore_signal(barrier, inc=1, device_id=(t // 2, 2 * z + t % 2), device_id_type=MESH)
        return carry

    def greet_ring(d, carry):
        t = lax.rem(z + d, nz)
        pl.semaphore_signal(barrier, inc=1, device_id=(w, 2 * t + c), device_id_type=MESH)
        return carry

    lax.fori_loop(1, 2 * n, greet_plane, 0)
    lax.fori_loop(1, nz, greet_ring, 0)
    pl.semaphore_wait(barrier, 2 * n - 1 + nz - 1)

    def gives(k):
        return jnp.logical_and(low, k < n2 - 1 - j)

    for k in range(n2 - 1):
        @pl.when(gives(k))
        def _():
            moved_tile(k, w + 2 + 2 * k).start()
    ask_copy.wait()

    def solve(i):
        @pl.when(i == 0)
        def _():
            diag_split_now()

        base_in.wait_recv()

        def add(col, acc):
            a, b = acc
            part_in(col, 0).wait_recv()
            part_in(col, 1).wait_recv()
            return a + partial[col, 0].astype(jnp.float32), b + partial[col, 1].astype(jnp.float32)

        zero = jnp.zeros((cols, half), jnp.float32)
        a, b = lax.fori_loop(0, i, add, (zero, zero))
        a = (base[0].astype(jnp.float32) - a).astype(jnp.bfloat16)
        b = (base[1].astype(jnp.float32) - b).astype(jnp.bfloat16)
        y = (dot_nt(a, diag_split[0]) + dot_nt(b, diag_split[1])).astype(jnp.bfloat16)
        sol[...] = y
        sol_split[0] = y[:, :half]
        sol_split[1] = y[:, half:]

        @pl.when(w < n2 - 1)
        def _():
            far_copy.start()

    def diag_split_now():
        diag_copy.wait()
        span, lane = 4 * rows * 2, 4 * rows
        m = lax.broadcasted_iota(jnp.int32, (span, span), 0)
        t = lax.broadcasted_iota(jnp.int32, (span, span), 1)
        core, t = t // lane, t % lane
        pick = (m == (t // rows) * (2 * rows) + core * rows + t % rows).astype(jnp.bfloat16)
        for u in range(diag.shape[1] // span):
            moved = jnp.dot(
                diag[:, u * span:(u + 1) * span], pick, preferred_element_type=jnp.float32
            ).astype(jnp.bfloat16)
            diag_split[0, :, u * lane:(u + 1) * lane] = moved[:, :lane]
            diag_split[1, :, u * lane:(u + 1) * lane] = moved[:, lane:]

    def apply(i, k, use_far):
        col = jnp.where(use_far, far, w)

        @pl.when(jnp.logical_and(use_far, k == 0))
        def _():
            far_copy.wait_recv()

        y = jnp.where(use_far, sol_far[...], sol[...])
        tile = gathered[k].reshape(half, gathered.shape[3])
        contrib[k] = dot_nt(y, tile).astype(jnp.bfloat16)
        part_copy(k, i, col, 0).start()
        part_copy(k, i, col, 1).start()

    def row_step(i):
        shared_end = first + 2 * (shared - 1)
        off = i - first
        near = jnp.logical_and(
            jnp.logical_and(off >= 0, i <= shared_end), lax.rem(off + 2 * n, 2) == 0
        )
        late = i > jnp.where(low, n - 1 - j, w)
        k = jnp.where(near, off // 2, i - jnp.where(low, n2, n2 + 1))
        k = jnp.where(jnp.logical_or(near, late), k, 0)

        @pl.when(jnp.logical_or(near, late))
        def _():
            apply(i, k, is_moved(k))

        @pl.when(i == w)
        def _():
            solve(i)

    def ring_slot(t):
        for m in range(hops // 2, -1, -1):
            k = t // 2 - m
            h = t % 2 + 2 * m
            live = jnp.logical_and(jnp.logical_and(k >= 0, k < count), h <= hops)

            @pl.when(jnp.logical_and(live, h == 0))
            def _():
                @pl.when(is_moved(k))
                def _():
                    moved_tile(k, 0).wait_recv()

                @pl.when(jnp.logical_not(is_moved(k)))
                def _():
                    local_tile(k).wait()

                ring_right(k, 0).start()
                ring_left(k, 0).start()

            @pl.when(jnp.logical_and(live, jnp.logical_and(h > 0, h < hops)))
            def _():
                ring_right_in(k, h - 1).wait_recv()
                ring_right(k, h).start()
                ring_left_in(k, h - 1).wait_recv()

                @pl.when(h < hops - 1)
                def _():
                    ring_left(k, h).start()

            @pl.when(jnp.logical_and(live, h == hops))
            def _():
                ring_right_in(k, h - 1).wait_recv()

    def ask_slot(t):
        @pl.when(t == 0)
        def _():
            ask_right(0).start()
            ask_left(0).start()

        @pl.when(jnp.logical_and(t > 0, t < hops))
        def _():
            ask_right_in(t - 1).wait_recv()
            ask_right(t).start()
            ask_left_in(t - 1).wait_recv()

            @pl.when(t < hops - 1)
            def _():
                ask_left(t).start()

        @pl.when(t == hops - 1)
        def _():
            ask_right_in(t).wait_recv()
            wide = asked.shape[2]
            pick = (
                lax.broadcasted_iota(jnp.int32, (cols, wide), 1)
                == cols * z + lax.broadcasted_iota(jnp.int32, (cols, wide), 0)
            ).astype(jnp.bfloat16)
            base[c] = dot_nt(pick, asked[...].reshape(half, wide)).astype(jnp.bfloat16)
            base_copy.start()

        @pl.when(jnp.logical_and(t == 2, w > 0))
        def _():
            diag_split_now()

    def slot(t, carry):
        ask_slot(t)
        ring_slot(t)
        i = t - (hops - 1)

        @pl.when(i >= 0)
        def _():
            row_step(i)

        return carry

    lax.fori_loop(0, n - 1 + hops, slot, 0)

    def out_copy(d):
        t = lax.rem(z + d, nz)
        return remote(sol_split.at[c], result.at[c, z], out_send.at[d], out_recv.at[d], (w, 2 * t + c))

    def out_in(d):
        t = lax.rem(z - d + nz, nz)
        return remote(sol_split.at[c], result.at[c, t], out_send.at[d], out_recv.at[d], (w, 2 * t + c))

    for d in range(1, hops + 1):
        out_copy(hops + 1 - d).start()
        if hops + d < nz:
            out_copy(hops + d).start()
    result[c, z] = sol_split[c]
    for d in range(1, nz):
        out_in(d).wait_recv()
    swap = remote(result.at[c], result.at[c], swap_send, swap_recv, (w, other))
    swap.start()

    for k in range(n2 - 1):
        @pl.when(gives(k))
        def _():
            moved_tile(k, w + 2 + 2 * k).wait_send()
    for k in range(n2):
        @pl.when(k < count)
        def _():
            for h in range(hops):
                ring_right(k, h).wait_send()
            for h in range(hops - 1):
                ring_left(k, h).wait_send()
            part_copy(k, 0, 0, 0).wait_send()
            part_copy(k, 0, 0, 1).wait_send()
    for h in range(hops):
        ask_right(h).wait_send()
    for h in range(hops - 1):
        ask_left(h).wait_send()
    base_copy.wait_send()

    @pl.when(w < n2 - 1)
    def _():
        far_copy.wait_send()

    for d in range(1, nz):
        out_copy(d).wait_send()
    swap.wait_send()
    remote(result.at[1 - c], result.at[1 - c], swap_send, swap_recv, (w, other)).wait_recv()
    for s in range(2):
        out[:, s * half:(s + 1) * half] = result[s].reshape(nz * cols, half)


def on_device(factor_tiles, inverse_blocks, demand):
    n, rows, _, _, width = factor_tiles.shape
    nz = lax.axis_size("pcol") // 2
    wide = demand.shape[2]
    cols = wide // nz
    half = width // 2
    n2, hops = n // 2, nz // 2
    dma = pltpu.SemaphoreType.DMA
    out = pl.pallas_call(
        functools.partial(kernel, n, nz, cols, rows),
        out_shape=jax.ShapeDtypeStruct((wide, width), jnp.bfloat16),
        in_specs=[pl.BlockSpec(memory_space=pl.ANY)] * 3,
        out_specs=pl.BlockSpec(memory_space=pltpu.VMEM),
        scratch_shapes=[
            pltpu.VMEM((n2, nz, rows, width), jnp.bfloat16),
            pltpu.VMEM((width, width), jnp.bfloat16),
            pltpu.VMEM((2, width, half), jnp.bfloat16),
            pltpu.VMEM((nz, rows, wide), jnp.bfloat16),
            pltpu.VMEM((2, cols, half), jnp.bfloat16),
            pltpu.VMEM((n, 2, cols, half), jnp.bfloat16),
            pltpu.VMEM((cols, width), jnp.bfloat16),
            pltpu.VMEM((2, cols, half), jnp.bfloat16),
            pltpu.VMEM((cols, width), jnp.bfloat16),
            pltpu.VMEM((n2, cols, half), jnp.bfloat16),
            pltpu.VMEM((2, nz, cols, half), jnp.bfloat16),
            dma((n2,)), dma((n2,)),
            dma((n2, hops)), dma((n2, hops)), dma((n2, hops - 1)), dma((n2, hops - 1)),
            dma, dma((hops,)), dma((hops,)), dma((hops - 1,)), dma((hops - 1,)),
            dma, dma, dma, dma((n2, 2)), dma((n, 2)),
            dma, dma, dma((nz,)), dma((nz,)), dma, dma,
        ],
        compiler_params=pltpu.CompilerParams(
            collective_id=0, has_side_effects=True, vmem_limit_bytes=48 * 1024 * 1024
        ),
    )(
        factor_tiles.reshape(n, rows, width),
        inverse_blocks.reshape(width, width),
        demand,
    )
    return out.T.reshape(1, 1, width, wide)


def solution(mesh):
    placed = (
        P(None, "pcol", None, "prow", None),
        P(None, "prow", None, None),
        P(None, "pcol", None),
    )
    return jax.shard_map(
        on_device,
        mesh=mesh,
        in_specs=placed,
        out_specs=P(None, "prow", None, None),
        check_vma=False,
    )
```

time: 1640 us -> 167 us (0.10)
  the two profiles are of different devices: /device:TPU:1 before, /device:TPU:31 now
where the time goes in v1:
time: 167 us
  Pallas kernels  162 us (97%)
  local copies, waits for them, and re-layouts  4.76 us (3%)
    pallas_call x1, Pallas kernels, on_device(): pl.pallas_call(functools.partial(kernel, n, nz, cols, rows), out_shape=ja...  162 us
    unnamed x6, local copies, waits for them, and re-layouts  3.76 us

profile of v1, /device:TPU:31, one launch (start us, length us, event | category | flops | bytes accessed | tf_op | source)
XLA Modules:
  0.0 166.8 jit_solution(2623837952973021968)
XLA Ops:
  0.0 0.0 copy-start
  0.0 1.6 copy-done
  1.6 0.0 copy-start.1
  1.6 1.2 copy-done.1
  2.8 0.0 copy-start.2
  2.8 0.9 copy-done.2
  3.8 162.0 %shard_map.37 = bf16[256,1024]{1,0:T(8,128)(2,1)S(1)} custom-call(bf16[16,32,1024]{2,1,0:T(8,128)(2,1)S(1)} %bitcast.7, bf16[1024,1024]{1,0:T(8,128)(2,1)S(1)} %bitcast.6, bf16[16,32,256]{2,1,0:T(8,128)(2,1)S(1)} %copy-done.2), custom_call_target="tpu_custom_call" | custom-call | tf_op jit(solution)/shard_map/pallas_call | solution.py:342
  165.8 1.0 copy.4
Async XLA Ops:
  0.0 1.6 copy-start
  1.6 1.2 copy-start.1
  2.8 0.9 copy-start.2

commit v2 on v1

--- a/solution.py
+++ b/solution.py
@@ -18,7 +18,7 @@
 def kernel(
     n, nz, cols, rows,
     tiles, inverse, demand, out,
-    gathered, diag, diag_split, asked, base, partial, sol, sol_split, sol_far, contrib, result,
+    gathered, diag, diag_split, asked, base, partial, sol, sol_split, sol_far, contrib, result, pick,
     own_sem, own_send, right_send, right_recv, left_send, left_recv,
     ask_own, ask_rsend, ask_rrecv, ask_lsend, ask_lrecv,
     diag_sem, base_send, base_recv, part_send, part_recv,
@@ -156,32 +156,43 @@
         sol_split[0] = y[:, :half]
         sol_split[1] = y[:, half:]
 
+        @pl.when(jnp.logical_and(i > 0, i < n - 1))
+        def _():
+            apply(i + 1, jnp.where(low, 0, i - n2), False)
+
         @pl.when(w < n2 - 1)
         def _():
             far_copy.start()
 
     def diag_split_now():
         diag_copy.wait()
-        span, lane = 4 * rows * 2, 4 * rows
-        m = lax.broadcasted_iota(jnp.int32, (span, span), 0)
-        t = lax.broadcasted_iota(jnp.int32, (span, span), 1)
-        core, t = t // lane, t % lane
-        pick = (m == (t // rows) * (2 * rows) + core * rows + t % rows).astype(jnp.bfloat16)
+        span, lane = 8 * rows, 4 * rows
+        m = lax.broadcasted_iota(jnp.int32, (2 * rows, rows), 0)
+        t = lax.broadcasted_iota(jnp.int32, (2 * rows, rows), 1)
+        pick[...] = jnp.zeros_like(pick)
+        for core in range(2):
+            unit = (m == t + core * rows).astype(jnp.bfloat16)
+            for b in range(4):
+                lo = core * lane + b * rows
+                pick[2 * rows * b:2 * rows * (b + 1), lo:lo + rows] = unit
         for u in range(diag.shape[1] // span):
             moved = jnp.dot(
-                diag[:, u * span:(u + 1) * span], pick, preferred_element_type=jnp.float32
+                diag[:, u * span:(u + 1) * span], pick[...], preferred_element_type=jnp.float32
             ).astype(jnp.bfloat16)
             diag_split[0, :, u * lane:(u + 1) * lane] = moved[:, :lane]
             diag_split[1, :, u * lane:(u + 1) * lane] = moved[:, lane:]
 
     def apply(i, k, use_far):
-        col = jnp.where(use_far, far, w)
-
-        @pl.when(jnp.logical_and(use_far, k == 0))
-        def _():
-            far_copy.wait_recv()
-
-        y = jnp.where(use_far, sol_far[...], sol[...])
+        if use_far is False:
+            col, y = w, sol[...]
+        else:
+            col = jnp.where(use_far, far, w)
+
+            @pl.when(jnp.logical_and(use_far, k == 0))
+            def _():
+                far_copy.wait_recv()
+
+            y = jnp.where(use_far, sol_far[...], sol[...])
         tile = gathered[k].reshape(half, gathered.shape[3])
         contrib[k] = dot_nt(y, tile).astype(jnp.bfloat16)
         part_copy(k, i, col, 0).start()
@@ -197,7 +208,9 @@
         k = jnp.where(near, off // 2, i - jnp.where(low, n2, n2 + 1))
         k = jnp.where(jnp.logical_or(near, late), k, 0)
 
-        @pl.when(jnp.logical_or(near, late))
+        done = jnp.logical_and(i == w + 1, w > 0)
+
+        @pl.when(jnp.logical_and(jnp.logical_or(near, late), jnp.logical_not(done)))
         def _():
             apply(i, k, is_moved(k))
 
@@ -258,11 +271,11 @@
         def _():
             ask_right_in(t).wait_recv()
             wide = asked.shape[2]
-            pick = (
+            mine = (
                 lax.broadcasted_iota(jnp.int32, (cols, wide), 1)
                 == cols * z + lax.broadcasted_iota(jnp.int32, (cols, wide), 0)
             ).astype(jnp.bfloat16)
-            base[c] = dot_nt(pick, asked[...].reshape(half, wide)).astype(jnp.bfloat16)
+            base[c] = dot_nt(mine, asked[...].reshape(half, wide)).astype(jnp.bfloat16)
             base_copy.start()
 
         @pl.when(jnp.logical_and(t == 2, w > 0))
@@ -342,7 +355,7 @@
     out = pl.pallas_call(
         functools.partial(kernel, n, nz, cols, rows),
         out_shape=jax.ShapeDtypeStruct((wide, width), jnp.bfloat16),
-        in_specs=[pl.BlockSpec(memory_space=pl.ANY)] * 3,
+        in_specs=[pl.BlockSpec(memory_space=pltpu.HBM)] * 3,
         out_specs=pl.BlockSpec(memory_space=pltpu.VMEM),
         scratch_shapes=[
             pltpu.VMEM((n2, nz, rows, width), jnp.bfloat16),
@@ -356,6 +369,7 @@
             pltpu.VMEM((cols, width), jnp.bfloat16),
             pltpu.VMEM((n2, cols, half), jnp.bfloat16),
             pltpu.VMEM((2, nz, cols, half), jnp.bfloat16),
+            pltpu.VMEM((8 * rows, 8 * rows), jnp.bfloat16),
             dma((n2,)), dma((n2,)),
             dma((n2, hops)), dma((n2, hops)), dma((n2, hops - 1)), dma((n2, hops - 1)),
             dma, dma((hops,)), dma((hops,)), dma((hops - 1,)), dma((hops - 1,)),

time: 167 us -> 168 us (level)
  no operation moved by 1% of the time
where the time goes in v2:
time: 168 us; the launch traced here: 167 us
  Pallas kernels  163 us (97%)
  local copies, waits for them, and re-layouts  4.76 us (3%)
    pallas_call x1, Pallas kernels, on_device(): pl.pallas_call(functools.partial(kernel, n, nz, cols, rows), out_shape=ja...  163 us
    unnamed x6, local copies, waits for them, and re-layouts  3.76 us

profile of v2, /device:TPU:31, one launch (start us, length us, event | category | flops | bytes accessed | tf_op | source)
XLA Modules:
  0.0 167.4 jit_solution(12518221540684168200)
XLA Ops:
  0.0 0.0 copy-start
  0.0 1.6 copy-done
  1.6 0.0 copy-start.1
  1.6 1.2 copy-done.1
  2.8 0.0 copy-start.2
  2.8 0.9 copy-done.2
  3.8 162.6 %shard_map.37 = bf16[256,1024]{1,0:T(8,128)(2,1)S(1)} custom-call(bf16[16,32,1024]{2,1,0:T(8,128)(2,1)S(1)} %bitcast.7, bf16[1024,1024]{1,0:T(8,128)(2,1)S(1)} %bitcast.6, bf16[16,32,256]{2,1,0:T(8,128)(2,1)S(1)} %copy-done.2), custom_call_target="tpu_custom_call" | custom-call | tf_op jit(solution)/shard_map/pallas_call | solution.py:355
  166.4 1.0 copy.4
Async XLA Ops:
  0.0 1.6 copy-start
  1.6 1.2 copy-start.1
  2.8 0.9 copy-start.2

commit v3 on v2

--- a/solution.py
+++ b/solution.py
@@ -29,8 +29,13 @@
     q = lax.axis_index("pcol")
     z, c = q // 2, q % 2
     other = q + 1 - 2 * c
-    right = lax.rem(z + 1, nz) * 2 + c
-    left = lax.rem(z + nz - 1, nz) * 2 + c
+    turn = 1 - 2 * c
+
+    def along(steps):
+        return lax.rem(z + turn * steps + nz, nz)
+
+    right = along(1) * 2 + c
+    left = along(-1) * 2 + c
     low = w < n2
     j = jnp.where(low, w, n - 1 - w)
     far = n - 1 - w
@@ -58,35 +63,35 @@
         return remote(tiles.at[row], gathered.at[k, z], own_send.at[k], own_sem.at[k], (far, q))
 
     def ring_right(k, h):
-        o = lax.rem(z - h + nz, nz)
+        o = along(-h)
         return remote(gathered.at[k, o], gathered.at[k, o], right_send.at[k, h], right_recv.at[k, h], (w, right))
 
     def ring_left(k, h):
-        o = lax.rem(z + h, nz)
+        o = along(h)
         return remote(gathered.at[k, o], gathered.at[k, o], left_send.at[k, h], left_recv.at[k, h], (w, left))
 
     def ring_right_in(k, h):
-        o = lax.rem(z - h - 1 + nz, nz)
+        o = along(-h - 1)
         return remote(gathered.at[k, o], gathered.at[k, o], right_send.at[k, h], right_recv.at[k, h], (w, right))
 
     def ring_left_in(k, h):
-        o = lax.rem(z + h + 1, nz)
+        o = along(h + 1)
         return remote(gathered.at[k, o], gathered.at[k, o], left_send.at[k, h], left_recv.at[k, h], (w, left))
 
     def ask_right(h):
-        o = lax.rem(z - h + nz, nz)
+        o = along(-h)
         return remote(asked.at[o], asked.at[o], ask_rsend.at[h], ask_rrecv.at[h], (w, right))
 
     def ask_left(h):
-        o = lax.rem(z + h, nz)
+        o = along(h)
         return remote(asked.at[o], asked.at[o], ask_lsend.at[h], ask_lrecv.at[h], (w, left))
 
     def ask_right_in(h):
-        o = lax.rem(z - h - 1 + nz, nz)
+        o = along(-h - 1)
         return remote(asked.at[o], asked.at[o], ask_rsend.at[h], ask_rrecv.at[h], (w, right))
 
     def ask_left_in(h):
-        o = lax.rem(z + h + 1, nz)
+        o = along(h + 1)
         return remote(asked.at[o], asked.at[o], ask_lsend.at[h], ask_lrecv.at[h], (w, left))
 
     base_copy = remote(base.at[c], base.at[c], base_send, base_recv, (w, other))
@@ -116,14 +121,26 @@
         pl.semaphore_signal(barrier, inc=1, device_id=(t // 2, 2 * z + t % 2), device_id_type=MESH)
         return carry
 
-    def greet_ring(d, carry):
-        t = lax.rem(z + d, nz)
-        pl.semaphore_signal(barrier, inc=1, device_id=(w, 2 * t + c), device_id_type=MESH)
-        return carry
-
     lax.fori_loop(1, 2 * n, greet_plane, 0)
-    lax.fori_loop(1, nz, greet_ring, 0)
-    pl.semaphore_wait(barrier, 2 * n - 1 + nz - 1)
+    for side in (right, left):
+        pl.semaphore_signal(barrier, inc=1, device_id=(w, side), device_id_type=MESH)
+    diag_copy.wait()
+    span, lane = 8 * rows, 4 * rows
+    m = lax.broadcasted_iota(jnp.int32, (2 * rows, rows), 0)
+    t = lax.broadcasted_iota(jnp.int32, (2 * rows, rows), 1)
+    pick[...] = jnp.zeros_like(pick)
+    for core in range(2):
+        unit = (m == t + core * rows).astype(jnp.bfloat16)
+        for b in range(4):
+            lo = core * lane + b * rows
+            pick[2 * rows * b:2 * rows * (b + 1), lo:lo + rows] = unit
+    for u in range(diag.shape[1] // span):
+        moved = jnp.dot(
+            diag[:, u * span:(u + 1) * span], pick[...], preferred_element_type=jnp.float32
+        ).astype(jnp.bfloat16)
+        diag_split[0, :, u * lane:(u + 1) * lane] = moved[:, :lane]
+        diag_split[1, :, u * lane:(u + 1) * lane] = moved[:, lane:]
+    pl.semaphore_wait(barrier, 2 * n - 1 + 2)
 
     def gives(k):
         return jnp.logical_and(low, k < n2 - 1 - j)
@@ -135,10 +152,6 @@
     ask_copy.wait()
 
     def solve(i):
-        @pl.when(i == 0)
-        def _():
-            diag_split_now()
-
         base_in.wait_recv()
 
         def add(col, acc):
@@ -164,24 +177,6 @@
         def _():
             far_copy.start()
 
-    def diag_split_now():
-        diag_copy.wait()
-        span, lane = 8 * rows, 4 * rows
-        m = lax.broadcasted_iota(jnp.int32, (2 * rows, rows), 0)
-        t = lax.broadcasted_iota(jnp.int32, (2 * rows, rows), 1)
-        pick[...] = jnp.zeros_like(pick)
-        for core in range(2):
-            unit = (m == t + core * rows).astype(jnp.bfloat16)
-            for b in range(4):
-                lo = core * lane + b * rows
-                pick[2 * rows * b:2 * rows * (b + 1), lo:lo + rows] = unit
-        for u in range(diag.shape[1] // span):
-            moved = jnp.dot(
-                diag[:, u * span:(u + 1) * span], pick[...], preferred_element_type=jnp.float32
-            ).astype(jnp.bfloat16)
-            diag_split[0, :, u * lane:(u + 1) * lane] = moved[:, :lane]
-            diag_split[1, :, u * lane:(u + 1) * lane] = moved[:, lane:]
-
     def apply(i, k, use_far):
         if use_far is False:
             col, y = w, sol[...]
@@ -193,6 +188,7 @@
                 far_copy.wait_recv()
 
             y = jnp.where(use_far, sol_far[...], sol[...])
+        ring_right_in(k, hops - 1).wait_recv()
         tile = gathered[k].reshape(half, gathered.shape[3])
         contrib[k] = dot_nt(y, tile).astype(jnp.bfloat16)
         part_copy(k, i, col, 0).start()
@@ -218,38 +214,30 @@
         def _():
             solve(i)
 
-    def ring_slot(t):
+    def ring_slot(u, parity):
         for m in range(hops // 2, -1, -1):
-            k = t // 2 - m
-            h = t % 2 + 2 * m
-            live = jnp.logical_and(jnp.logical_and(k >= 0, k < count), h <= hops)
-
-            @pl.when(jnp.logical_and(live, h == 0))
-            def _():
-                @pl.when(is_moved(k))
-                def _():
-                    moved_tile(k, 0).wait_recv()
-
-                @pl.when(jnp.logical_not(is_moved(k)))
-                def _():
-                    local_tile(k).wait()
-
-                ring_right(k, 0).start()
-                ring_left(k, 0).start()
-
-            @pl.when(jnp.logical_and(live, jnp.logical_and(h > 0, h < hops)))
-            def _():
-                ring_right_in(k, h - 1).wait_recv()
+            h = parity + 2 * m
+            if h >= hops:
+                continue
+            k = u - m
+
+            @pl.when(jnp.logical_and(k >= 0, k < count))
+            def _():
+                if h == 0:
+                    @pl.when(is_moved(k))
+                    def _():
+                        moved_tile(k, 0).wait_recv()
+
+                    @pl.when(jnp.logical_not(is_moved(k)))
+                    def _():
+                        local_tile(k).wait()
+                else:
+                    ring_right_in(k, h - 1).wait_recv()
                 ring_right(k, h).start()
-                ring_left_in(k, h - 1).wait_recv()
-
-                @pl.when(h < hops - 1)
-                def _():
+                if h > 0:
+                    ring_left_in(k, h - 1).wait_recv()
+                if h < hops - 1:
                     ring_left(k, h).start()
-
-            @pl.when(jnp.logical_and(live, h == hops))
-            def _():
-                ring_right_in(k, h - 1).wait_recv()
 
     def ask_slot(t):
         @pl.when(t == 0)
@@ -278,22 +266,24 @@
             base[c] = dot_nt(mine, asked[...].reshape(half, wide)).astype(jnp.bfloat16)
             base_copy.start()
 
-        @pl.when(jnp.logical_and(t == 2, w > 0))
-        def _():
-            diag_split_now()
-
-    def slot(t, carry):
-        ask_slot(t)
-        ring_slot(t)
-        i = t - (hops - 1)
-
-        @pl.when(i >= 0)
-        def _():
-            row_step(i)
+    def slot_pair(u, carry):
+        for parity in range(2):
+            t = 2 * u + parity
+
+            @pl.when(t < hops)
+            def _():
+                ask_slot(t)
+
+            ring_slot(u, parity)
+            i = t - (hops - 1)
+
+            @pl.when(jnp.logical_and(i >= 0, i < n))
+            def _():
+                row_step(i)
 
         return carry
 
-    lax.fori_loop(0, n - 1 + hops, slot, 0)
+    lax.fori_loop(0, (n + hops) // 2, slot_pair, 0)
 
     def out_copy(d):
         t = lax.rem(z + d, nz)
@@ -377,7 +367,7 @@
             dma, dma, dma((nz,)), dma((nz,)), dma, dma,
         ],
         compiler_params=pltpu.CompilerParams(
-            collective_id=0, has_side_effects=True, vmem_limit_bytes=48 * 1024 * 1024
+            collective_id=0, has_side_effects=True
         ),
     )(
         factor_tiles.reshape(n, rows, width),

time: 168 us -> 161 us (0.958)
  Pallas kernels: 163 us -> 159 us
  local copies, waits for them, and re-layouts: 4.76 us -> 2.04 us
    unnamed x6 -> x0, local copies, waits for them, and re-layouts: 3.76 us -> none
    pallas_call x1, Pallas kernels: 163 us -> 159 us  [on_device(): pl.pallas_call(functools.partial(kernel, n, nz, cols, rows), out_shape=ja...]
where the time goes in v3:
time: 161 us
  Pallas kernels  159 us (99%)
  local copies, waits for them, and re-layouts  2.04 us (1%)
    pallas_call x1, Pallas kernels, on_device(): pl.pallas_call(functools.partial(kernel, n, nz, cols, rows), out_shape=ja...  159 us

profile of v3, /device:TPU:31, one launch (start us, length us, event | category | flops | bytes accessed | tf_op | source)
XLA Modules:
  0.0 161.2 jit_solution(7887788227987054642)
XLA Ops:
  0.0 159.1 %shard_map.37 = bf16[256,1024]{1,0:T(8,128)(2,1)} custom-call(bf16[16,32,1024]{2,1,0:T(8,128)(2,1)} %bitcast.7, bf16[1024,1024]{1,0:T(8,128)(2,1)} %bitcast.6, bf16[16,32,256]{2,1,0:T(8,128)(2,1)} %demand.1), custom_call_target="tpu_custom_call" | custom-call | tf_op jit(solution)/shard_map/pallas_call | solution.py:345
  159.1 2.0 %copy.4 = bf16[1,1,1024,256]{3,2,1,0:T(8,128)(2,1)} copy(bf16[1,1,1024,256]{2,3,1,0:T(8,128)(2,1)} %bitcast.5) | data formatting | bytes 1048576 | tf_op jit(solution)/shard_map/reshape | solution.py:377

commit v4 on v3

--- a/solution.py
+++ b/solution.py
@@ -41,7 +41,7 @@
     far = n - 1 - w
     count = jnp.where(low, n2, n2 - 1)
     shared = jnp.where(low, n2 - j, n2 - 1 - j)
-    first = jnp.where(low, j + 1, j + 2)
+    span_j = n - 1 - 2 * j
     half = gathered.shape[1] * rows
 
     def remote(src, dst, send, recv, device):
@@ -51,7 +51,10 @@
         )
 
     def row_of(k):
-        return jnp.where(k < shared, first + 2 * k, jnp.where(low, n2, n2 + 1) + k)
+        own = jnp.where(k == 0, 1, jnp.where(k == shared - 1, span_j, 2 * k))
+        moved = jnp.where(k == shared - 1, span_j - 1, 2 * k + 3)
+        near = j + jnp.where(low, own, moved)
+        return jnp.where(k < shared, near, jnp.where(low, n2, n2 + 1) + k)
 
     def is_moved(k):
         return jnp.logical_and(jnp.logical_not(low), k < shared)
@@ -148,7 +151,7 @@
     for k in range(n2 - 1):
         @pl.when(gives(k))
         def _():
-            moved_tile(k, w + 2 + 2 * k).start()
+            moved_tile(k, w + jnp.where(k == n2 - 2 - j, span_j - 1, 2 * k + 3)).start()
     ask_copy.wait()
 
     def solve(i):
@@ -169,50 +172,48 @@
         sol_split[0] = y[:, :half]
         sol_split[1] = y[:, half:]
 
-        @pl.when(jnp.logical_and(i > 0, i < n - 1))
-        def _():
-            apply(i + 1, jnp.where(low, 0, i - n2), False)
-
         @pl.when(w < n2 - 1)
         def _():
             far_copy.start()
 
-    def apply(i, k, use_far):
-        if use_far is False:
-            col, y = w, sol[...]
-        else:
-            col = jnp.where(use_far, far, w)
-
-            @pl.when(jnp.logical_and(use_far, k == 0))
-            def _():
-                far_copy.wait_recv()
-
-            y = jnp.where(use_far, sol_far[...], sol[...])
+    def apply(k, use_far):
+        col = jnp.where(use_far, far, w)
+        y = jnp.where(use_far, sol_far[...], sol[...])
         ring_right_in(k, hops - 1).wait_recv()
         tile = gathered[k].reshape(half, gathered.shape[3])
         contrib[k] = dot_nt(y, tile).astype(jnp.bfloat16)
-        part_copy(k, i, col, 0).start()
-        part_copy(k, i, col, 1).start()
+        row = row_of(k)
+        part_copy(k, row, col, 0).start()
+        part_copy(k, row, col, 1).start()
 
     def row_step(i):
-        shared_end = first + 2 * (shared - 1)
-        off = i - first
-        near = jnp.logical_and(
-            jnp.logical_and(off >= 0, i <= shared_end), lax.rem(off + 2 * n, 2) == 0
+        last = i // 2
+        own_event = i == w
+        far_event = jnp.logical_and(jnp.logical_not(low), jnp.logical_and(i == j + 2, shared > 0))
+        since = jnp.where(is_moved(last), j + 2, w)
+        ready = jnp.logical_and(lax.rem(i, 2) == 0, jnp.logical_and(last < count, i > since))
+        start = jnp.where(own_event, jnp.where(low, 0, shared), jnp.where(far_event, 0, last))
+        stop = jnp.where(
+            own_event,
+            jnp.minimum(last, count - 1),
+            jnp.where(far_event, jnp.minimum(last, shared - 1), jnp.where(ready, last, start - 1)),
         )
-        late = i > jnp.where(low, n - 1 - j, w)
-        k = jnp.where(near, off // 2, i - jnp.where(low, n2, n2 + 1))
-        k = jnp.where(jnp.logical_or(near, late), k, 0)
-
-        done = jnp.logical_and(i == w + 1, w > 0)
-
-        @pl.when(jnp.logical_and(jnp.logical_or(near, late), jnp.logical_not(done)))
-        def _():
-            apply(i, k, is_moved(k))
-
-        @pl.when(i == w)
+
+        @pl.when(own_event)
         def _():
             solve(i)
+
+        @pl.when(far_event)
+        def _():
+            far_copy.wait_recv()
+
+        use_far = is_moved(start)
+
+        def step(k, carry):
+            apply(k, use_far)
+            return carry
+
+        lax.fori_loop(start, stop + 1, step, 0)
 
     def ring_slot(u, parity):
         for m in range(hops // 2, -1, -1):
@@ -306,7 +307,7 @@
     for k in range(n2 - 1):
         @pl.when(gives(k))
         def _():
-            moved_tile(k, w + 2 + 2 * k).wait_send()
+            moved_tile(k, w + jnp.where(k == n2 - 2 - j, span_j - 1, 2 * k + 3)).wait_send()
     for k in range(n2):
         @pl.when(k < count)
         def _():

time: 161 us -> 155 us (0.963)
  Pallas kernels: 159 us -> 152 us
    pallas_call x1, Pallas kernels: 159 us -> 152 us  [on_device(): pl.pallas_call(functools.partial(kernel, n, nz, cols, rows), out_shape=ja...]
where the time goes in v4:
time: 155 us; the launch traced here: 154 us
  Pallas kernels  152 us (98%)
  local copies, waits for them, and re-layouts  2.04 us (1%)
    pallas_call x1, Pallas kernels, on_device(): pl.pallas_call(functools.partial(kernel, n, nz, cols, rows), out_shape=ja...  152 us

profile of v4, /device:TPU:31, one launch (start us, length us, event | category | flops | bytes accessed | tf_op | source)
XLA Modules:
  0.0 154.3 jit_solution(7787820860629369817)
XLA Ops:
  0.0 152.3 %shard_map.37 = bf16[256,1024]{1,0:T(8,128)(2,1)} custom-call(bf16[16,32,1024]{2,1,0:T(8,128)(2,1)} %bitcast.7, bf16[1024,1024]{1,0:T(8,128)(2,1)} %bitcast.6, bf16[16,32,256]{2,1,0:T(8,128)(2,1)} %demand.1), custom_call_target="tpu_custom_call" | custom-call | tf_op jit(solution)/shard_map/pallas_call | solution.py:346
  152.3 2.0 %copy.4 = bf16[1,1,1024,256]{3,2,1,0:T(8,128)(2,1)} copy(bf16[1,1,1024,256]{2,3,1,0:T(8,128)(2,1)} %bitcast.5) | data formatting | bytes 1048576 | tf_op jit(solution)/shard_map/reshape | solution.py:378

commit v5 on v4

--- a/solution.py
+++ b/solution.py
@@ -288,19 +288,35 @@
 
     def out_copy(d):
         t = lax.rem(z + d, nz)
-        return remote(sol_split.at[c], result.at[c, z], out_send.at[d], out_recv.at[d], (w, 2 * t + c))
+        spot = result.at[c, z // 4, z % 4]
+        return remote(sol_split.at[c], spot, out_send.at[d], out_recv.at[d], (w, 2 * t + c))
 
     def out_in(d):
         t = lax.rem(z - d + nz, nz)
-        return remote(sol_split.at[c], result.at[c, t], out_send.at[d], out_recv.at[d], (w, 2 * t + c))
-
-    for d in range(1, hops + 1):
-        out_copy(hops + 1 - d).start()
-        if hops + d < nz:
-            out_copy(hops + d).start()
-    result[c, z] = sol_split[c]
-    for d in range(1, nz):
+        spot = result.at[c, t // 4, t % 4]
+        return remote(sol_split.at[c], spot, out_send.at[d], out_recv.at[d], (w, 2 * t + c))
+
+    def group_copy(d):
+        mine = result.at[c, :, z % 4]
+        t = lax.rem(z + d, nz)
+        return remote(mine, mine, out_send.at[d], out_recv.at[d], (w, 2 * t + c))
+
+    def group_in(d):
+        t = lax.rem(z - d + nz, nz)
+        theirs = result.at[c, :, t % 4]
+        return remote(theirs, theirs, out_send.at[d], out_recv.at[d], (w, 2 * z + 1 - c))
+
+    strides = sorted(range(4, nz, 4), key=lambda d: -min(d, nz - d))
+    nears = (2, 1, nz - 1)
+    for d in strides:
+        out_copy(d).start()
+    result[c, z // 4, z % 4] = sol_split[c]
+    for d in strides:
         out_in(d).wait_recv()
+    for d in nears:
+        group_copy(d).start()
+    for d in nears:
+        group_in(d).wait_recv()
     swap = remote(result.at[c], result.at[c], swap_send, swap_recv, (w, other))
     swap.start()
 
@@ -327,8 +343,10 @@
     def _():
         far_copy.wait_send()
 
-    for d in range(1, nz):
+    for d in strides:
         out_copy(d).wait_send()
+    for d in nears:
+        group_copy(d).wait_send()
     swap.wait_send()
     remote(result.at[1 - c], result.at[1 - c], swap_send, swap_recv, (w, other)).wait_recv()
     for s in range(2):
@@ -359,7 +377,7 @@
             pltpu.VMEM((2, cols, half), jnp.bfloat16),
             pltpu.VMEM((cols, width), jnp.bfloat16),
             pltpu.VMEM((n2, cols, half), jnp.bfloat16),
-            pltpu.VMEM((2, nz, cols, half), jnp.bfloat16),
+            pltpu.VMEM((2, nz // 4, 4, cols, half), jnp.bfloat16),
             pltpu.VMEM((8 * rows, 8 * rows), jnp.bfloat16),
             dma((n2,)), dma((n2,)),
             dma((n2, hops)), dma((n2, hops)), dma((n2, hops - 1)), dma((n2, hops - 1)),

time: 155 us -> 151 us (0.974)
  Pallas kernels: 152 us -> 149 us
    pallas_call x1, Pallas kernels: 152 us -> 149 us  [on_device(): pl.pallas_call(functools.partial(kernel, n, nz, cols, rows), out_shape=ja...]
where the time goes in v5:
time: 151 us
  Pallas kernels  149 us (99%)
  local copies, waits for them, and re-layouts  2.04 us (1%)
    pallas_call x1, Pallas kernels, on_device(): pl.pallas_call(functools.partial(kernel, n, nz, cols, rows), out_shape=ja...  149 us

profile of v5, /device:TPU:31, one launch (start us, length us, event | category | flops | bytes accessed | tf_op | source)
XLA Modules:
  0.0 150.7 jit_solution(11959079371231360386)
XLA Ops:
  0.0 148.7 %shard_map.37 = bf16[256,1024]{1,0:T(8,128)(2,1)} custom-call(bf16[16,32,1024]{2,1,0:T(8,128)(2,1)} %bitcast.7, bf16[1024,1024]{1,0:T(8,128)(2,1)} %bitcast.6, bf16[16,32,256]{2,1,0:T(8,128)(2,1)} %demand.1), custom_call_target="tpu_custom_call" | custom-call | tf_op jit(solution)/shard_map/pallas_call | solution.py:364
  148.7 2.0 %copy.4 = bf16[1,1,1024,256]{3,2,1,0:T(8,128)(2,1)} copy(bf16[1,1,1024,256]{2,3,1,0:T(8,128)(2,1)} %bitcast.5) | data formatting | bytes 1048576 | tf_op jit(solution)/shard_map/reshape | solution.py:396
